TPU v7x, 128 devices: a whole 4x4x4 slice. The times are simulated.
128 devices in a mesh: row: 8 (over z, core), col: 16 (over x, y).
Axes of the slice: x: 4, y: 4, z: 4, core: 2. Of those that a mesh axis runs over, the one named last changes fastest.
Arguments:
- tokens: bfloat16 [2048, 4096], P('row', 'col'), may hold values from -6 to 6
- lengths: int32 [64], P('col'), may hold values from 1 to 64, as said below
- adapter_ids: int32 [64], P('col'), may hold values from 0 to 255, as said below
- adapter_place: int32 [256], replicated, may hold values from 0 to 255, as said below
- attention_qkv_weight: bfloat16 [2048, 6144], P('col', 'row'), may hold values from -0.125 to 0.125
- attention_out_weight: bfloat16 [2048, 2048], P('col', 'row'), may hold values from -0.125 to 0.125
- widen_weight: bfloat16 [2048, 8192], P('col', 'row'), may hold values from -0.125 to 0.125
- contract_weight: bfloat16 [2048, 8192], P('col', 'row'), may hold values from -0.0625 to 0.0625
- first_gain: float32 [2048], P('row'), may hold values from 0.5 to 1.5
- first_shift: float32 [2048], replicated, may hold values from -3 to 3
- second_gain: float32 [2048], replicated, may hold values from 0.5 to 1.5
- second_shift: float32 [2048], replicated, may hold values from -3 to 3
- attend_shrink: bfloat16 [256, 192, 2048], P('col', None, 'row'), may hold values from -0.125 to 0.125
- attend_expand: bfloat16 [256, 3, 64, 2048], P('col', None, None, 'row'), may hold values from -0.75 to 0.75
- output_shrink: bfloat16 [256, 64, 2048], P('col', None, 'row'), may hold values from -0.125 to 0.125
- output_expand: bfloat16 [256, 64, 2048], P('col', None, 'row'), may hold values from -0.75 to 0.75
- upward_shrink: bfloat16 [256, 64, 2048], P('col', None, 'row'), may hold values from -0.125 to 0.125
- upward_expand: bfloat16 [256, 64, 8192], P('col', None, 'row'), may hold values from -0.75 to 0.75
- downward_shrink: bfloat16 [256, 64, 8192], P('col', None, 'row'), may hold values from -0.0625 to 0.0625
- downward_expand: bfloat16 [256, 64, 2048], P('col', None, 'row'), may hold values from -0.75 to 0.75
Outputs:
- layer_out: bfloat16 [2048, 4096], P(None, 'col')
Inputs may be any that keep to these rules, and one draw needn't show every extreme that they name: `lengths`: each aligned block of 4 requests holds a prompt of exactly 64 tokens. `adapter_ids`: in each aligned block of 4 requests, at most 2 name adapters whose store positions lie in one aligned block of 16 positions, and exactly 2 do for some such block. `adapter_place`: A permutation.
All inputs are finite; a program needn't handle non-finite values.
Results may differ from a plain program's by a relative error of at most 0.024.
Values may be sent and summed in bfloat16 or wider, within the bound.
A program may use at most 128 MiB of HBM per device.

v0:
```python
import math
import jax
import jax.numpy as jnp
from jax import lax
from jax.sharding import PartitionSpec as P

D = 2048
HD = 128
CAP = 2
eps = 1e-12
lowrank_scale = 0.5


def fold_weight(shard, combine, initial):
    return combine(initial, lax.all_gather(shard, "col", axis=0, tiled=True), jnp.int32(0))


def project(shard, full_rows):
    initial = jnp.zeros((shard.shape[1], full_rows.shape[1]), jnp.float32)

    def accumulate(total, piece, start):
        return lax.dot_general(
            piece, full_rows, (((0,), (0,)), ((), ())), preferred_element_type=jnp.float32
        )

    return fold_weight(shard, accumulate, initial)


def gather_rows(shard):
    return lax.all_gather(shard, "row", axis=0, tiled=True)


def row_total(value):
    return lax.psum(value.astype(jnp.bfloat16), "row").astype(jnp.float32)


def route_tables(adapter_ids, adapter_place, stored, columns, capacity):
    total_adapters = adapter_place.shape[0]
    match = adapter_ids[:, None] == jnp.arange(total_adapters, dtype=jnp.int32)[None, :]
    position = jnp.sum(jnp.where(match, adapter_place[None, :], 0), axis=1)
    owner = position // stored
    local = position % stored
    count = adapter_ids.shape[0]
    earlier = jnp.arange(count)[None, :] < jnp.arange(count)[:, None]
    same_owner = owner[None, :] == owner[:, None]
    rank = jnp.sum(jnp.where(earlier & same_owner, 1, 0), axis=1).astype(jnp.int32)
    select = (owner[None, None, :] == jnp.arange(columns, dtype=jnp.int32)[:, None, None]) & (
        rank[None, None, :] == jnp.arange(capacity, dtype=jnp.int32)[None, :, None]
    )
    slot_ids = jnp.sum(jnp.where(select, local[None, None, :] + 1, 0), axis=2) - 1
    return (select.astype(jnp.bfloat16), slot_ids)


def expanded_base(expand, reduced):
    return jnp.einsum("ockp,ocks->opcs", expand, reduced, preferred_element_type=jnp.float32)


def expanded_combined(expand, reduced):
    columns, capacity, three, rank, width = expand.shape
    slot = reduced.shape[3]
    grouped = reduced.reshape(columns, capacity, three, rank, slot)
    part = jnp.einsum("ocjkp,ocjks->ojpcs", expand, grouped, preferred_element_type=jnp.float32)
    part = part.reshape(columns, three, width // HD, HD, capacity, slot)
    part = part.transpose(0, 2, 1, 3, 4, 5)
    return part.reshape(columns, three * width, capacity, slot)


def pack_slots(inputs, select):
    columns, capacity, requests = select.shape
    width = inputs.shape[0]
    slot = inputs.shape[1] // requests
    blocks = inputs.reshape(width, requests, slot)
    return jnp.einsum("okj,ijs->oiks", select, blocks, preferred_element_type=jnp.float32).astype(
        jnp.bfloat16
    )


def apply_slots(arrived, shrink, expand, expand_rule):
    partial_result = jnp.einsum(
        "ocki,oics->ocks", shrink, arrived, preferred_element_type=jnp.float32
    )
    reduced = row_total(partial_result).astype(jnp.bfloat16)
    return expand_rule(expand, reduced).astype(jnp.bfloat16)


def unpack_slots(returned, select):
    out_width = returned.shape[1]
    home = jnp.einsum("okj,opks->pjs", select, returned, preferred_element_type=jnp.float32)
    return home.reshape(out_width, -1)


def sent_delta(inputs, select, slot_ids, shrink_store, expand_store, expand_rule):
    packed = pack_slots(inputs, select)
    columns, width, capacity, slot = packed.shape
    arrived, arrived_ids = (
        lax.all_to_all(
            packed.reshape(columns, width, capacity * slot),
            "col",
            split_axis=0,
            concat_axis=0,
            tiled=True,
        ),
        lax.all_to_all(slot_ids, "col", split_axis=0, concat_axis=0, tiled=True),
    )
    arrived = arrived.reshape(columns, width, capacity, slot)
    safe_ids = jnp.maximum(arrived_ids, 0)
    lowrank_update = apply_slots(
        arrived,
        jnp.take(shrink_store, safe_ids, axis=0),
        jnp.take(expand_store, safe_ids, axis=0),
        expand_rule,
    )
    out_width = lowrank_update.shape[1]
    returned = lax.all_to_all(
        lowrank_update.reshape(columns, out_width, capacity * slot),
        "col",
        split_axis=0,
        concat_axis=0,
        tiled=True,
    )
    return unpack_slots(returned.reshape(columns, out_width, capacity, slot), select)


def layer_norm_shard(values, gain, shift):
    sums = row_total(jnp.stack([jnp.sum(values, axis=0), jnp.sum(values * values, axis=0)]))
    mean = sums[0] / D
    square_mean = sums[1] / D
    factor = lax.rsqrt(square_mean - mean * mean + eps)
    return (values - mean) * factor * gain[:, None] + shift[:, None]


def shards(
    tokens,
    lengths,
    adapter_ids,
    adapter_place,
    attention_qkv_weight,
    attention_out_weight,
    widen_weight,
    contract_weight,
    first_gain,
    first_shift,
    second_gain,
    second_shift,
    attend_shrink,
    attend_expand,
    output_shrink,
    output_expand,
    upward_shrink,
    upward_expand,
    downward_shrink,
    downward_expand,
):
    columns = lax.axis_size("col")
    stored = attend_shrink.shape[0]
    select, slot_ids = route_tables(adapter_ids, adapter_place, stored, columns, CAP)
    requests = adapter_ids.shape[0]
    width_portion, token_count = tokens.shape
    slot = token_count // requests
    column_offset = lax.axis_index("row") * width_portion
    stores = (
        (attend_shrink, attend_expand),
        (output_shrink, output_expand),
        (upward_shrink, upward_expand),
        (downward_shrink, downward_expand),
    )

    def adapter_contribution(number, inputs, expand_rule):
        return sent_delta(
            inputs, select, slot_ids, stores[number][0], stores[number][1], expand_rule
        )

    full_tokens = gather_rows(tokens)
    combined_parts = project(attention_qkv_weight, full_tokens)
    combined_parts = combined_parts + lowrank_scale * adapter_contribution(
        0, tokens, expanded_combined
    )
    combined_parts = combined_parts.astype(jnp.bfloat16).reshape(-1, 3, HD, requests, slot)
    query = combined_parts[:, 0]
    keys = combined_parts[:, 1]
    values = combined_parts[:, 2]
    scores = jnp.einsum(
        "hdrq,hdrk->hrqk", query, keys, preferred_element_type=jnp.float32
    ) / math.sqrt(HD)
    valid = jnp.arange(slot, dtype=jnp.int32)[None, :] < lengths[:, None]
    weights = jnp.where(valid[None, :, None, :], jnp.exp(scores), 0.0)
    probs = (weights / jnp.sum(weights, axis=3, keepdims=True)).astype(jnp.bfloat16)
    attended_context = jnp.einsum(
        "hdrk,hrqk->hdrq", values, probs, preferred_element_type=jnp.float32
    )
    attended_context = attended_context.astype(jnp.bfloat16).reshape(-1, token_count)
    full_context = gather_rows(attended_context)
    attention_mixed = project(attention_out_weight, full_context)
    attention_mixed = attention_mixed + lowrank_scale * adapter_contribution(
        1, attended_context, expanded_base
    )
    first_residual_input = tokens.astype(jnp.float32) + attention_mixed
    first_norm_output = layer_norm_shard(
        first_residual_input,
        first_gain,
        lax.dynamic_slice_in_dim(first_shift, column_offset, width_portion, 0),
    ).astype(jnp.bfloat16)
    full_first = gather_rows(first_norm_output)
    hidden_units = project(widen_weight, full_first)
    hidden_units = hidden_units + lowrank_scale * adapter_contribution(
        2, first_norm_output, expanded_base
    )
    hidden_units = jax.nn.gelu(hidden_units, approximate=True).astype(jnp.bfloat16)
    initial = jnp.zeros((D, token_count), jnp.float32)

    def place_rows(total, piece, start):
        return jnp.dot(piece, hidden_units, preferred_element_type=jnp.float32)

    partial_result = fold_weight(contract_weight, place_rows, initial)
    downward_update = adapter_contribution(3, hidden_units, expanded_base)
    own_rows = (
        lax.dynamic_slice_in_dim(partial_result, column_offset, width_portion, 0)
        + lowrank_scale * downward_update
    )
    partial_result = lax.dynamic_update_slice_in_dim(partial_result, own_rows, column_offset, 0)
    summed = row_total(partial_result)
    second_residual_input = full_first.astype(jnp.float32) + summed
    mean = jnp.mean(second_residual_input, axis=0)
    square_mean = jnp.mean(second_residual_input * second_residual_input, axis=0)
    factor = lax.rsqrt(square_mean - mean * mean + eps)
    result = (second_residual_input - mean) * factor * second_gain[:, None] + second_shift[:, None]
    return result.astype(jnp.bfloat16)


def solution(mesh):
    return jax.shard_map(
        shards,
        mesh=mesh,
        in_specs=(
            P("row", "col"),
            P("col"),
            P("col"),
            P(),
            P("col", "row"),
            P("col", "row"),
            P("col", "row"),
            P("col", "row"),
            P("row"),
            P(),
            P(),
            P(),
            P("col", None, "row"),
            P("col", None, None, "row"),
            P("col", None, "row"),
            P("col", None, "row"),
            P("col", None, "row"),
            P("col", None, "row"),
            P("col", None, "row"),
            P("col", None, "row"),
        ),
        out_specs=P(None, "col"),
        check_vma=False,
    )
```

profile of v0, /device:TPU:0, one launch (start us, length us, event | category | flops | bytes accessed | tf_op | source)
XLA Modules:
  0.0 916.0 jit_solution(4494370504113886302)
XLA Ops:
  8.6 7.1 all-to-all-start
  31.0 11.9 %all-to-all-done.1 = bf16[16,256,128]{1,2,0:T(8,128)(2,1)S(1)} async-done(((bf16[16,256,128]{1,2,0:T(8,128)(2,1)}), bf16[16,256,128]{1,2,0:T(8,128)(2,1)S(1)}, u32[]{:S(2)}, u32[]{:S(2)}) %all-to-all-start.1) | async-done | bytes 1048608 | tf_op jit(solution)/shard_map/all_to_all | solution.py:96
  57.5 58.0 %all-reduce.6.cloned.1.call-done = bf16[16,2,3,64,64]{3,4,1,2,0:T(8,128)(2,1)} async-done(((bf16[16,2,3,64,64]{3,4,1,2,0:T(8,128)(2,1)}), bf16[16,2,3,64,64]{3,4,1,2,0:T(8,128)(2,1)}) %all-reduce.6.cloned.1.call-update) | async-done | bytes 786448 | tf_op jit(solution)/shard_map/psum | solution.py:34
  115.6 5.2 convert_bitcast_fusion.1
  120.8 5.5 convert_element_type.122
  126.2 9.3 %copy.256 = bf16[16,3,2,128,2,64]{3,1,2,5,4,0:T(4,128)(2,1)} copy(bf16[16,3,2,128,2,64]{3,2,5,4,1,0:T(2,128)(2,1)} %convert_element_type.122) | data formatting | bytes 6291456 | tf_op jit(solution)/shard_map/convert_element_type | solution.py:83
  135.5 8.9 convert_element_type.124
  144.4 7.5 all-to-all-start.2
  152.6 42.9 %all-to-all-done.2 = bf16[16,768,128]{1,2,0:T(8,128)(2,1)} async-done(((bf16[16,768,128]{1,2,0:T(8,128)(2,1)}), bf16[16,768,128]{1,2,0:T(8,128)(2,1)}, u32[]{:S(2)}, u32[]{:S(2)}) %all-to-all-start.2) | async-done | bytes 3145760 | tf_op jit(solution)/shard_map/all_to_all | solution.py:114
  200.6 20.6 %all-gather.8.cloned.1.call-done = bf16[2048,768]{1,0:T(8,128)(2,1)} async-done(((bf16[128,768]{1,0:T(8,128)(2,1)}), bf16[2048,768]{1,0:T(8,128)(2,1)}) %all-gather.8.cloned.1.call-update) | async-done | bytes 3145744 | tf_op jit(solution)/shard_map/all_gather | solution.py:15
  239.4 15.2 %all-to-all-done.3 = bf16[16,256,128]{1,2,0:T(8,128)(2,1)} async-done(((bf16[16,256,128]{1,2,0:T(8,128)(2,1)}), bf16[16,256,128]{1,2,0:T(8,128)(2,1)}, u32[]{:S(2)}, u32[]{:S(2)}) %all-to-all-start.3) | async-done | bytes 1048608 | tf_op jit(solution)/shard_map/all_to_all | solution.py:96
  260.6 55.9 %all-reduce.8.cloned.1.call-done = bf16[16,2,64,64]{3,2,1,0:T(8,128)(2,1)} async-done(((bf16[16,2,64,64]{3,2,1,0:T(8,128)(2,1)}), bf16[16,2,64,64]{3,2,1,0:T(8,128)(2,1)}) %all-reduce.8.cloned.1.call-update) | async-done | bytes 262160 | tf_op jit(solution)/shard_map/psum | solution.py:34
  319.1 6.9 all-to-all-start.4
  326.8 15.3 %all-to-all-done.4 = bf16[16,256,128]{1,2,0:T(8,128)(2,1)S(1)} async-done(((bf16[16,256,128]{1,2,0:T(8,128)(2,1)}), bf16[16,256,128]{1,2,0:T(8,128)(2,1)S(1)}, u32[]{:S(2)}, u32[]{:S(2)}) %all-to-all-start.4) | async-done | bytes 1048608 | tf_op jit(solution)/shard_map/all_to_all | solution.py:114
  342.8 22.0 %all-gather.14.cloned.1.call-done = bf16[2048,256]{1,0:T(8,128)(2,1)} async-done(((bf16[128,256]{1,0:T(8,128)(2,1)}), bf16[2048,256]{1,0:T(8,128)(2,1)}) %all-gather.14.cloned.1.call-update) | async-done | bytes 1048592 | tf_op jit(solution)/shard_map/all_gather | solution.py:15
  364.8 24.4 %all-gather.12.cloned.1.call-done = bf16[2048,256]{0,1:T(8,128)(2,1)} async-done(((bf16[256,256]{0,1:T(8,128)(2,1)}), bf16[2048,256]{0,1:T(8,128)(2,1)}) %all-gather.12.cloned.1.call-update) | async-done | bytes 1048592 | tf_op jit(solution)/shard_map/all_gather | solution.py:30
  391.4 14.4 %psum.44 = bf16[2,256]{1,0:T(2,128)(2,1)S(1)} all-reduce(bf16[2,256]{1,0:T(2,128)(2,1)S(1)} %pad_maximum_fusion), channel_id=1, replica_groups=mesh['row'=8,'col'=16] {'row'}, use_global_device_ids=true, to_apply=%region_8.10 | all-reduce | flops 512 | bytes 2048 | tf_op jit(solution)/shard_map/psum | solution.py:34
  408.1 6.9 all-to-all-start.5
  416.6 13.7 %all-to-all-done.5 = bf16[16,256,128]{1,2,0:T(8,128)(2,1)} async-done(((bf16[16,256,128]{1,2,0:T(8,128)(2,1)}), bf16[16,256,128]{1,2,0:T(8,128)(2,1)}, u32[]{:S(2)}, u32[]{:S(2)}) %all-to-all-start.5) | async-done | bytes 1048608 | tf_op jit(solution)/shard_map/all_to_all | solution.py:96
  436.8 55.5 %all-reduce.10.cloned.1.call-done = bf16[16,2,64,64]{3,2,1,0:T(8,128)(2,1)} async-done(((bf16[16,2,64,64]{3,2,1,0:T(8,128)(2,1)}), bf16[16,2,64,64]{3,2,1,0:T(8,128)(2,1)}) %all-reduce.10.cloned.1.call-update) | async-done | bytes 262160 | tf_op jit(solution)/shard_map/psum | solution.py:34
  492.4 5.7 fusion.15
  498.0 6.9 all-to-all-start.6
  505.6 56.7 %all-to-all-done.6 = bf16[16,1024,128]{1,2,0:T(8,128)(2,1)} async-done(((bf16[16,1024,128]{1,2,0:T(8,128)(2,1)}), bf16[16,1024,128]{1,2,0:T(8,128)(2,1)}, u32[]{:S(2)}, u32[]{:S(2)}) %all-to-all-start.6) | async-done | bytes 4194336 | tf_op jit(solution)/shard_map/all_to_all | solution.py:114
  567.6 24.0 %all-gather.18.cloned.1.call-done = bf16[2048,1024]{1,0:T(8,128)(2,1)} async-done(((bf16[128,1024]{1,0:T(8,128)(2,1)}), bf16[2048,1024]{1,0:T(8,128)(2,1)}) %all-gather.18.cloned.1.call-update) | async-done | bytes 4194320 | tf_op jit(solution)/shard_map/all_gather | solution.py:15
  591.6 31.3 %all-gather.16.cloned.1.call-done = bf16[2048,256]{0,1:T(8,128)(2,1)} async-done(((bf16[256,256]{0,1:T(8,128)(2,1)}), bf16[2048,256]{0,1:T(8,128)(2,1)}) %all-gather.16.cloned.1.call-update) | async-done | bytes 1048592 | tf_op jit(solution)/shard_map/all_gather | solution.py:30
  632.8 7.0 all-to-all-start.7
  642.7 53.2 %all-to-all-done.7 = bf16[16,1024,128]{1,2,0:T(8,128)(2,1)} async-done(((bf16[16,1024,128]{1,2,0:T(8,128)(2,1)}), bf16[16,1024,128]{1,2,0:T(8,128)(2,1)}, u32[]{:S(2)}, u32[]{:S(2)}) %all-to-all-start.7) | async-done | bytes 4194336 | tf_op jit(solution)/shard_map/all_to_all | solution.py:96
  695.9 5.6 fusion.38
  703.0 68.0 %all-reduce.12.cloned.1.call-done = bf16[16,2,64,64]{3,2,1,0:T(8,128)(2,1)} async-done(((bf16[16,2,64,64]{3,2,1,0:T(8,128)(2,1)}), bf16[16,2,64,64]{3,2,1,0:T(8,128)(2,1)}) %all-reduce.12.cloned.1.call-update) | async-done | bytes 262160 | tf_op jit(solution)/shard_map/psum | solution.py:34
  773.5 6.8 all-to-all-start.8
  780.3 48.7 %all-gather.20.cloned.1.call-done = bf16[2048,1024]{1,0:T(8,128)(2,1)} async-done(((bf16[128,1024]{1,0:T(8,128)(2,1)}), bf16[2048,1024]{1,0:T(8,128)(2,1)}) %all-gather.20.cloned.1.call-update) | async-done | bytes 4194320 | tf_op jit(solution)/shard_map/all_gather | solution.py:15
  839.3 62.7 %all-reduce.14.cloned.1.call-done = bf16[2048,256]{0,1:T(8,128)(2,1)} async-done(((bf16[2048,256]{0,1:T(8,128)(2,1)}), bf16[2048,256]{0,1:T(8,128)(2,1)}) %all-reduce.14.cloned.1.call-update) | async-done | bytes 1048592 | tf_op jit(solution)/shard_map/psum | solution.py:34
  (143 shorter events, 118.0 us)
Async XLA Ops:
  6.5 427.4 %copy-start = (bf16[16,64,1024]{2,1,0:T(8,128)(2,1)S(1)}, bf16[16,64,1024]{2,1,0:T(8,128)(2,1)}, u32[]{:S(2)}) copy-start(bf16[16,64,1024]{2,1,0:T(8,128)(2,1)} %param.41) | copy-start | bytes 6291460
  8.6 14.6 %all-to-all-start = ((s32[16,1,2]{2,1,0:T(1,128)}), s32[16,1,2]{2,1,0:T(1,128)S(1)}, u32[]{:S(2)}, u32[]{:S(2)}) async-start(s32[16,1,2]{2,1,0:T(1,128)} %copy.149), calls=%async_computation | async-start | bytes 16384 | tf_op jit(solution)/shard_map/all_to_all | solution.py:103
  23.2 19.7 %all-to-all-start.1 = ((bf16[16,256,128]{1,2,0:T(8,128)(2,1)}), bf16[16,256,128]{1,2,0:T(8,128)(2,1)S(1)}, u32[]{:S(2)}, u32[]{:S(2)}) async-start(bf16[16,256,128]{1,2,0:T(8,128)(2,1)} %copy.154), calls=%async_computation.1 | async-start | bytes 2097152 | tf_op jit(solution)/shard_map/all_to_all | solution.py:96
  26.9 88.7 %all-reduce.6.cloned.1.call-start = ((), (), s32[]{:S(2)}) async-start(), calls=%async_computation.11 | async-start | bytes 3145728 | tf_op jit(solution)/shard_map/psum | solution.py:34
  52.2 148.4 %all-gather.10.cloned.1.call-start = ((), (), s32[]{:S(2)}) async-start(), calls=%async_computation.10 | async-start | bytes 1179648 | tf_op jit(solution)/shard_map/all_gather | solution.py:30
  52.9 168.3 %all-gather.8.cloned.1.call-start = ((), (), s32[]{:S(2)}) async-start(), calls=%async_computation.9 | async-start | bytes 3342336 | tf_op jit(solution)/shard_map/all_gather | solution.py:15
  144.4 7.5 copy-start.15
  144.4 51.0 %all-to-all-start.2 = ((bf16[16,768,128]{1,2,0:T(8,128)(2,1)}), bf16[16,768,128]{1,2,0:T(8,128)(2,1)}, u32[]{:S(2)}, u32[]{:S(2)}) async-start(bf16[16,768,128]{1,2,0:T(8,128)(2,1)} %convert_element_type.124), calls=%async_computation.2 | async-start | bytes 6291456 | tf_op jit(solution)/shard_map/all_to_all | solution.py:114
  230.7 7.1 copy-start.5
  233.1 21.5 %all-to-all-start.3 = ((bf16[16,256,128]{1,2,0:T(8,128)(2,1)}), bf16[16,256,128]{1,2,0:T(8,128)(2,1)}, u32[]{:S(2)}, u32[]{:S(2)}) async-start(bf16[16,256,128]{1,2,0:T(8,128)(2,1)} %bitcast.27), calls=%async_computation.3 | async-start | bytes 2097152 | tf_op jit(solution)/shard_map/all_to_all | solution.py:96
  237.5 79.0 %all-reduce.8.cloned.1.call-start = ((), (), s32[]{:S(2)}) async-start(), calls=%async_computation.14 | async-start | bytes 1048576 | tf_op jit(solution)/shard_map/psum | solution.py:34
  257.5 107.4 %all-gather.14.cloned.1.call-start = ((), (), s32[]{:S(2)}) async-start(), calls=%async_computation.13 | async-start | bytes 1114112 | tf_op jit(solution)/shard_map/all_gather | solution.py:15
  258.0 131.2 %all-gather.12.cloned.1.call-start = ((), (), s32[]{:S(2)}) async-start(), calls=%async_computation.12 | async-start | bytes 1179648 | tf_op jit(solution)/shard_map/all_gather | solution.py:30
  319.1 86.7 %copy-start.14 = (f32[256]{0:T(256)S(1)}, f32[256]{0:T(256)}, u32[]{:S(2)}) copy-start(f32[256]{0:T(256)} %param.32) | copy-start | bytes 3076
  319.1 23.0 %all-to-all-start.4 = ((bf16[16,256,128]{1,2,0:T(8,128)(2,1)}), bf16[16,256,128]{1,2,0:T(8,128)(2,1)S(1)}, u32[]{:S(2)}, u32[]{:S(2)}) async-start(bf16[16,256,128]{1,2,0:T(8,128)(2,1)} %bitcast.31), calls=%async_computation.4 | async-start | bytes 2097152 | tf_op jit(solution)/shard_map/all_to_all | solution.py:114
  391.4 23.6 %copy-start.6 = (bf16[16,64,256]{2,1,0:T(8,128)(2,1)S(1)}, bf16[16,64,256]{2,1,0:T(8,128)(2,1)}, u32[]{:S(2)}) copy-start(bf16[16,64,256]{2,1,0:T(8,128)(2,1)} %param.40) | copy-start | bytes 1572868
  405.9 10.6 %copy-start.8 = (bf16[256,256]{0,1:T(8,128)(2,1)}, bf16[256,256]{0,1:T(8,128)(2,1)S(1)}, u32[]{:S(2)}) copy-start(bf16[256,256]{0,1:T(8,128)(2,1)S(1)} %add_convert_fusion.1) | copy-start | bytes 393220
  408.1 22.3 %all-to-all-start.5 = ((bf16[16,256,128]{1,2,0:T(8,128)(2,1)}), bf16[16,256,128]{1,2,0:T(8,128)(2,1)}, u32[]{:S(2)}, u32[]{:S(2)}) async-start(bf16[16,256,128]{1,2,0:T(8,128)(2,1)} %bitcast.44), calls=%async_computation.5 | async-start | bytes 2097152 | tf_op jit(solution)/shard_map/all_to_all | solution.py:96
  414.9 77.4 %all-reduce.10.cloned.1.call-start = ((), (), s32[]{:S(2)}) async-start(), calls=%async_computation.17 | async-start | bytes 1048576 | tf_op jit(solution)/shard_map/psum | solution.py:34
  433.2 158.4 %all-gather.18.cloned.1.call-start = ((), (), s32[]{:S(2)}) async-start(), calls=%async_computation.16 | async-start | bytes 4456448 | tf_op jit(solution)/shard_map/all_gather | solution.py:15
  498.0 64.3 %all-to-all-start.6 = ((bf16[16,1024,128]{1,2,0:T(8,128)(2,1)}), bf16[16,1024,128]{1,2,0:T(8,128)(2,1)}, u32[]{:S(2)}, u32[]{:S(2)}) async-start(bf16[16,1024,128]{1,2,0:T(8,128)(2,1)} %bitcast.185), calls=%async_computation.6 | async-start | bytes 8388608 | tf_op jit(solution)/shard_map/all_to_all | solution.py:114
  504.9 118.0 %all-gather.16.cloned.1.call-start = ((), (), s32[]{:S(2)}) async-start(), calls=%async_computation.15 | async-start | bytes 1179648 | tf_op jit(solution)/shard_map/all_gather | solution.py:30
  632.8 7.0 copy-start.2
  632.8 63.2 %all-to-all-start.7 = ((bf16[16,1024,128]{1,2,0:T(8,128)(2,1)}), bf16[16,1024,128]{1,2,0:T(8,128)(2,1)}, u32[]{:S(2)}, u32[]{:S(2)}) async-start(bf16[16,1024,128]{1,2,0:T(8,128)(2,1)} %bitcast.186), calls=%async_computation.7 | async-start | bytes 8388608 | tf_op jit(solution)/shard_map/all_to_all | solution.py:96
  639.8 131.2 %all-reduce.12.cloned.1.call-start = ((), (), s32[]{:S(2)}) async-start(), calls=%async_computation.19 | async-start | bytes 1048576 | tf_op jit(solution)/shard_map/psum | solution.py:34
  701.6 127.5 %all-gather.20.cloned.1.call-start = ((), (), s32[]{:S(2)}) async-start(), calls=%async_computation.18 | async-start | bytes 4456448 | tf_op jit(solution)/shard_map/all_gather | solution.py:15
  702.3 126.7 %copy-start.11 = (bf16[1024,256]{0,1:T(8,128)(2,1)S(1)}, bf16[1024,256]{0,1:T(8,128)(2,1)}, u32[]{:S(2)}) copy-start(bf16[1024,256]{0,1:T(8,128)(2,1)} %copy-done.10) | copy-start | bytes 1572868
  773.5 60.6 %all-to-all-start.8 = ((bf16[16,256,128]{1,2,0:T(8,128)(2,1)}), bf16[16,256,128]{1,2,0:T(8,128)(2,1)S(1)}, u32[]{:S(2)}, u32[]{:S(2)}) async-start(bf16[16,256,128]{1,2,0:T(8,128)(2,1)} %bitcast.64), calls=%async_computation.8 | async-start | bytes 2097152 | tf_op jit(solution)/shard_map/all_to_all | solution.py:114
  780.3 121.7 %all-reduce.14.cloned.1.call-start = ((), (), s32[]{:S(2)}) async-start(), calls=%async_computation.20 | async-start | bytes 2097152 | tf_op jit(solution)/shard_map/psum | solution.py:34
  835.0 67.0 %copy-start.3 = (bf16[2048,256]{0,1:T(8,128)(2,1)S(1)}, bf16[2048,256]{0,1:T(8,128)(2,1)}, u32[]{:S(2)}) copy-start(bf16[2048,256]{0,1:T(8,128)(2,1)} %all-gather.16.cloned.1.call-done) | copy-start | bytes 3145732
  838.1 65.8 %copy-start.12 = (f32[2048]{0:T(1024)S(1)}, f32[2048]{0:T(1024)}, u32[]{:S(2)}) copy-start(f32[2048]{0:T(1024)} %param.35) | copy-start | bytes 24580
  838.1 65.8 %copy-start.13 = (f32[2048]{0:T(1024)S(1)}, f32[2048]{0:T(1024)}, u32[]{:S(2)}) copy-start(f32[2048]{0:T(1024)} %param.34) | copy-start | bytes 24580
  (5 other events, 21.5 us)
Sparse Core Ops, SparseCore 0:
  52.3 63.2 all-reduce.5
  117.3 22.7 all-gather.9
  142.3 78.8 all-gather.7
  257.6 58.9 all-reduce.7
  318.5 46.2 all-gather.13
  366.3 22.8 all-gather.11
  433.3 59.0 all-reduce.9
  494.5 97.0 all-gather.17
  593.3 29.5 all-gather.15
  701.7 69.2 all-reduce.11
  773.1 55.9 all-gather.19
  839.4 62.5 all-reduce.13
where the time goes:
time: 926 us; the launch traced here: 916 us
  waiting for transfers between devices  688 us (74%)
  local copies, waits for them, and re-layouts  71.5 us (8%)
  matrix products  60.5 us (7%)
  starting transfers between devices  58 us (6%)
  blocking collectives  14.4 us (2%)
  between operations  14.3 us (2%)
    psum x5, waiting for transfers between devices, row_total(): return lax.psum(value.astype(jnp.bfloat16), 'row').astype(jnp.float32)  300 us
    all_gather x4, waiting for transfers between devices, fold_weight(): lax.all_gather(shard, 'col', axis=0, tiled=True)  115 us
    all_to_all x4, waiting for transfers between devices, sent_delta(): lax.all_to_all(lowrank_update.reshape(columns, out_width, capacity * slot...  115 us
    all_to_all x4, waiting for transfers between devices, sent_delta(): lax.all_to_all(packed.reshape(columns, width, capacity * slot), 'col', sp...  94.1 us
    all_gather x3, waiting for transfers between devices, gather_rows(): return lax.all_gather(shard, 'row', axis=0, tiled=True)  55.8 us
    all_to_all x4, starting transfers between devices, sent_delta(): lax.all_to_all(lowrank_update.reshape(columns, out_width, capacity * slot...  28.1 us
    convert_element_type x3, local copies, waits for them, and re-layouts, apply_slots(): return expand_rule(expand, reduced).astype(jnp.bfloat16)  23.7 us
    all_to_all x4, starting transfers between devices, sent_delta(): lax.all_to_all(packed.reshape(columns, width, capacity * slot), 'col', sp...  21.9 us
  transfers between devices with their start and end apart: 21, of which 19 were waited for; matrix products, arithmetic and copies ran while one was open for 9% of the time, Pallas kernels for 0%

commit v1 on v0

--- a/solution.py
+++ b/solution.py
@@ -11,8 +11,21 @@
 lowrank_scale = 0.5
 
 
+def collect(value, axis, dim):
+    ways = lax.axis_size(axis)
+    up = [(d, (d + 1) % ways) for d in range(ways)]
+    down = [(d, (d - 1) % ways) for d in range(ways)]
+    earlier, later = ([value], [value])
+    for _ in range(ways // 2):
+        earlier.append(lax.ppermute(earlier[-1], axis, up))
+    for _ in range((ways - 1) // 2):
+        later.append(lax.ppermute(later[-1], axis, down))
+    line = jnp.concatenate([*earlier[::-1], *later[1:]], axis=dim)
+    return jnp.roll(line, (lax.axis_index(axis) - ways // 2) * value.shape[dim], axis=dim)
+
+
 def fold_weight(shard, combine, initial):
-    return combine(initial, lax.all_gather(shard, "col", axis=0, tiled=True), jnp.int32(0))
+    return combine(initial, collect(shard, "col", 0), jnp.int32(0))
 
 
 def project(shard, full_rows):

time: 926 us -> 968 us (1.045)
  waiting for transfers between devices: 688 us -> 447 us
  starting transfers between devices: 58 us -> 208 us
  local copies, waits for them, and re-layouts: 71.5 us -> 195 us
    ppermute x0 -> x60, waiting for transfers between devices: none -> 179 us  [the longest x32 172 us: collect(): earlier.append(lax.ppermute(earlier[-1], axis, up))]
    ppermute x0 -> x60, starting transfers between devices: none -> 150 us  [the longest x28 139 us: collect(): later.append(lax.ppermute(later[-1], axis, down))]
    all_gather x4 -> x0, waiting for transfers between devices: 115 us -> none  [fold_weight(): lax.all_gather(shard, 'col', axis=0, tiled=True)]
    unnamed x38 -> x211, local copies, waits for them, and re-layouts: 5.59 us -> 117 us
    all_to_all x4, waiting for transfers between devices: 115 us -> 5.99 us  [sent_delta(): lax.all_to_all(lowrank_update.reshape(columns, out_width, capacity * slot...]
    psum x5, waiting for transfers between devices: 300 us -> 229 us  [row_total(): return lax.psum(value.astype(jnp.bfloat16), 'row').astype(jnp.float32)]
    all_to_all x4, waiting for transfers between devices: 94.1 us -> 24.4 us  [sent_delta(): lax.all_to_all(packed.reshape(columns, width, capacity * slot), 'col', sp...]
    all_gather x3, waiting for transfers between devices: 55.8 us -> 4 us  [gather_rows(): return lax.all_gather(shard, 'row', axis=0, tiled=True)]
  transfers between devices with their start and end apart: 21 -> 77, of which waited for: 19 -> 41; matrix products, arithmetic and copies ran while one was open for 9% -> 24% of each run, Pallas kernels for 0% -> 0%
where the time goes in v1:
time: 968 us; the launch traced here: 956 us
  waiting for transfers between devices  447 us (46%)
  starting transfers between devices  208 us (21%)
  local copies, waits for them, and re-layouts  195 us (20%)
  matrix products  65.7 us (7%)
  blocking collectives  15.6 us (2%)
  between operations  14.7 us (2%)
  other arithmetic  9.91 us (1%)
    psum x5, waiting for transfers between devices, row_total(): return lax.psum(value.astype(jnp.bfloat16), 'row').astype(jnp.float32)  229 us
    ppermute x32, waiting for transfers between devices, collect(): earlier.append(lax.ppermute(earlier[-1], axis, up))  172 us
    ppermute x28, starting transfers between devices, collect(): later.append(lax.ppermute(later[-1], axis, down))  139 us
    unnamed x211, local copies, waits for them, and re-layouts  117 us
    all_to_all x4, starting transfers between devices, sent_delta(): lax.all_to_all(lowrank_update.reshape(columns, out_width, capacity * slot...  27.7 us
    all_to_all x4, waiting for transfers between devices, sent_delta(): lax.all_to_all(packed.reshape(columns, width, capacity * slot), 'col', sp...  24.4 us
    convert_element_type x3, local copies, waits for them, and re-layouts, apply_slots(): return expand_rule(expand, reduced).astype(jnp.bfloat16)  23.6 us
    all_to_all x4, starting transfers between devices, sent_delta(): lax.all_to_all(packed.reshape(columns, width, capacity * slot), 'col', sp...  22.4 us
  transfers between devices with their start and end apart: 77, of which 41 were waited for; matrix products, arithmetic and copies ran while one was open for 24% of the time, Pallas kernels for 0%

profile of v1, /device:TPU:0, one launch (start us, length us, event | category | flops | bytes accessed | tf_op | source)
XLA Modules:
  0.0 955.6 jit_solution(4823535391511917481)
XLA Ops:
  8.6 7.1 all-to-all-start
  33.9 9.2 all-to-all-done.1
  79.4 5.8 collective-permute-start.11
  87.1 5.9 collective-permute-start.12
  135.5 5.8 collective-permute-start.27
  144.8 5.8 collective-permute-start.28
  153.8 5.9 collective-permute-start.29
  170.3 9.2 copy.265
  179.5 8.9 convert_element_type.124
  188.5 7.2 all-to-all-start.2
  263.9 7.4 all-to-all-start.3
  294.5 55.2 %all-reduce.8.cloned.1.call-done = bf16[16,2,64,64]{3,2,1,0:T(8,128)(2,1)} async-done(((bf16[16,2,64,64]{3,2,1,0:T(8,128)(2,1)}), bf16[16,2,64,64]{3,2,1,0:T(8,128)(2,1)}) %all-reduce.8.cloned.1.call-update) | async-done | bytes 262160 | tf_op jit(solution)/shard_map/psum | solution.py:47
  352.2 6.8 all-to-all-start.4
  377.1 15.6 %psum.44 = bf16[2,256]{1,0:T(2,128)(2,1)S(1)} all-reduce(bf16[2,256]{1,0:T(2,128)(2,1)S(1)} %pad_maximum_fusion), channel_id=1, replica_groups=mesh['row'=8,'col'=16] {'row'}, use_global_device_ids=true, to_apply=%region_8.10 | all-reduce | flops 512 | bytes 2048 | tf_op jit(solution)/shard_map/psum | solution.py:47
  402.0 13.8 %all-to-all-done.5 = bf16[16,256,128]{1,2,0:T(8,128)(2,1)} async-done(((bf16[16,256,128]{1,2,0:T(8,128)(2,1)}), bf16[16,256,128]{1,2,0:T(8,128)(2,1)}, u32[]{:S(2)}, u32[]{:S(2)}) %all-to-all-start.5) | async-done | bytes 1048608 | tf_op jit(solution)/shard_map/all_to_all | solution.py:109
  422.2 55.5 %all-reduce.10.cloned.1.call-done = bf16[16,2,64,64]{3,2,1,0:T(8,128)(2,1)} async-done(((bf16[16,2,64,64]{3,2,1,0:T(8,128)(2,1)}), bf16[16,2,64,64]{3,2,1,0:T(8,128)(2,1)}) %all-reduce.10.cloned.1.call-update) | async-done | bytes 262160 | tf_op jit(solution)/shard_map/psum | solution.py:47
  477.7 5.7 fusion.23
  483.4 6.9 all-to-all-start.6
  495.8 50.1 %collective-permute-done.46 = bf16[128,1024]{1,0:T(8,128)(2,1)S(1)} collective-permute-done((bf16[128,1024]{1,0:T(8,128)(2,1)S(1)}, bf16[128,1024]{1,0:T(8,128)(2,1)S(1)}, u32[]{:S(2)}, u32[]{:S(2)}) %collective-permute-start.46) | collective-permute-done | bytes 262176 | tf_op jit(solution)/shard_map/ppermute | solution.py:20
  581.4 6.5 collective-permute-done.50
  593.2 6.6 collective-permute-done.51
  599.9 5.7 collective-permute-start.59
  641.4 7.0 all-to-all-start.7
  650.4 57.3 %collective-permute-done.30 = bf16[128,1024]{1,0:T(8,128)(2,1)S(1)} collective-permute-done((bf16[128,1024]{1,0:T(8,128)(2,1)S(1)}, bf16[128,1024]{1,0:T(8,128)(2,1)S(1)}, u32[]{:S(2)}, u32[]{:S(2)}) %collective-permute-start.30) | collective-permute-done | bytes 262176 | tf_op jit(solution)/shard_map/ppermute | solution.py:20
  728.2 5.8 collective-permute-start.40
  738.6 5.8 collective-permute-start.41
  748.3 5.8 collective-permute-start.42
  758.4 5.9 collective-permute-start.43
  788.6 5.6 fusion.48
  795.7 56.0 %all-reduce.12.cloned.1.call-done = bf16[16,2,64,64]{3,2,1,0:T(8,128)(2,1)} async-done(((bf16[16,2,64,64]{3,2,1,0:T(8,128)(2,1)}), bf16[16,2,64,64]{3,2,1,0:T(8,128)(2,1)}) %all-reduce.12.cloned.1.call-update) | async-done | bytes 262160 | tf_op jit(solution)/shard_map/psum | solution.py:47
  854.2 6.9 all-to-all-start.8
  879.6 61.9 %all-reduce.14.cloned.1.call-done = bf16[2048,256]{0,1:T(8,128)(2,1)} async-done(((bf16[2048,256]{0,1:T(8,128)(2,1)}), bf16[2048,256]{0,1:T(8,128)(2,1)}) %all-reduce.14.cloned.1.call-update) | async-done | bytes 1048592 | tf_op jit(solution)/shard_map/psum | solution.py:47
  (427 shorter events, 416.3 us)
Async XLA Ops:
  23.4 19.7 %all-to-all-start.1 = ((bf16[16,256,128]{1,2,0:T(8,128)(2,1)}), bf16[16,256,128]{1,2,0:T(8,128)(2,1)S(1)}, u32[]{:S(2)}, u32[]{:S(2)}) async-start(bf16[16,256,128]{1,2,0:T(8,128)(2,1)} %copy.160), calls=%async_computation.1 | async-start | bytes 2097152 | tf_op jit(solution)/shard_map/all_to_all | solution.py:109
  27.0 132.7 %all-reduce.6.cloned.1.call-start = ((), (), s32[]{:S(2)}) async-start(), calls=%async_computation.10 | async-start | bytes 3145728 | tf_op jit(solution)/shard_map/psum | solution.py:47
  27.1 26.6 %collective-permute-start = (bf16[128,256]{1,0:T(8,128)(2,1)S(1)}, bf16[128,256]{1,0:T(8,128)(2,1)}, u32[]{:S(2)}, u32[]{:S(2)}) collective-permute-start(bf16[128,256]{1,0:T(8,128)(2,1)S(1)} %copy-done.43), channel_id=1, source_target_pairs={{0,1},{1,2},{2,3},{3,4},{4,5},{5,6},{6,7},{7,8},{8,9},{9,10},{10,1... | collective-permute-start | bytes 196616 | tf_op jit(solution)/shard_map/ppermute | solution.py:20
  52.3 191.3 %all-gather.4.cloned.1.call-start = ((), (), s32[]{:S(2)}) async-start(), calls=%async_computation.9 | async-start | bytes 1179648 | tf_op jit(solution)/shard_map/all_gather | solution.py:43
  52.4 22.8 %collective-permute-start.15 = (bf16[128,768]{1,0:T(8,128)(2,1)S(1)}, bf16[128,768]{1,0:T(8,128)(2,1)S(1)}, u32[]{:S(2)}, u32[]{:S(2)}) collective-permute-start(bf16[128,768]{1,0:T(8,128)(2,1)S(1)} %copy-done.8), channel_id=1, source_target_pairs={{0,1},{1,2},{2,3},{3,4},{4,5},{5,6},{6,7},{7,8},{8,9},{9,10},{10,1... | collective-permute-start | bytes 589832 | tf_op jit(solution)/shard_map/ppermute | solution.py:20
  69.7 24.3 %collective-permute-start.23 = (bf16[128,768]{1,0:T(8,128)(2,1)S(1)}, bf16[128,768]{1,0:T(8,128)(2,1)}, u32[]{:S(2)}, u32[]{:S(2)}) collective-permute-start(bf16[128,768]{1,0:T(8,128)(2,1)S(1)} %copy-done.8), channel_id=1, source_target_pairs={{0,15},{1,0},{2,1},{3,2},{4,3},{5,4},{6,5},{7,6},{8,7},{9,8},{10,9... | collective-permute-start | bytes 589832 | tf_op jit(solution)/shard_map/ppermute | solution.py:22
  75.2 26.1 %collective-permute-start.16 = (bf16[128,768]{1,0:T(8,128)(2,1)S(1)}, bf16[128,768]{1,0:T(8,128)(2,1)}, u32[]{:S(2)}, u32[]{:S(2)}) collective-permute-start(bf16[128,768]{1,0:T(8,128)(2,1)S(1)} %collective-permute-done.15), channel_id=1, source_target_pairs={{0,1},{1,2},{2,3},{3,4},{4,5},{5,6},{6,7},{7,8},{8,9},{9,10},{10,1... | collective-permute-start | bytes 589832 | tf_op jit(solution)/shard_map/ppermute | solution.py:20
  94.1 18.5 %collective-permute-start.24 = (bf16[128,768]{1,0:T(8,128)(2,1)}, bf16[128,768]{1,0:T(8,128)(2,1)}, u32[]{:S(2)}, u32[]{:S(2)}) collective-permute-start(bf16[128,768]{1,0:T(8,128)(2,1)} %collective-permute-done.23), channel_id=1, source_target_pairs={{0,15},{1,0},{2,1},{3,2},{4,3},{5,4},{6,5},{7,6},{8,7},{9,8},{10,9... | collective-permute-start | bytes 589832 | tf_op jit(solution)/shard_map/ppermute | solution.py:22
  99.5 18.5 %collective-permute-start.13 = (bf16[128,256]{1,0:T(8,128)(2,1)}, bf16[128,256]{1,0:T(8,128)(2,1)}, u32[]{:S(2)}, u32[]{:S(2)}) collective-permute-start(bf16[128,256]{1,0:T(8,128)(2,1)} %collective-permute-done.12), channel_id=1, source_target_pairs={{0,15},{1,0},{2,1},{3,2},{4,3},{5,4},{6,5},{7,6},{8,7},{9,8},{10,9... | collective-permute-start | bytes 196616 | tf_op jit(solution)/shard_map/ppermute | solution.py:22
  101.3 19.6 %collective-permute-start.17 = (bf16[128,768]{1,0:T(8,128)(2,1)}, bf16[128,768]{1,0:T(8,128)(2,1)}, u32[]{:S(2)}, u32[]{:S(2)}) collective-permute-start(bf16[128,768]{1,0:T(8,128)(2,1)} %collective-permute-done.16), channel_id=1, source_target_pairs={{0,1},{1,2},{2,3},{3,4},{4,5},{5,6},{6,7},{7,8},{8,9},{9,10},{10,1... | collective-permute-start | bytes 589832 | tf_op jit(solution)/shard_map/ppermute | solution.py:20
  118.0 160.4 %collective-permute-start.14 = (bf16[128,256]{1,0:T(8,128)(2,1)}, bf16[128,256]{1,0:T(8,128)(2,1)}, u32[]{:S(2)}, u32[]{:S(2)}) collective-permute-start(bf16[128,256]{1,0:T(8,128)(2,1)} %collective-permute-done.13), channel_id=1, source_target_pairs={{0,15},{1,0},{2,1},{3,2},{4,3},{5,4},{6,5},{7,6},{8,7},{9,8},{10,9... | collective-permute-start | bytes 196616 | tf_op jit(solution)/shard_map/ppermute | solution.py:22
  153.8 62.7 %collective-permute-start.29 = (bf16[128,768]{1,0:T(8,128)(2,1)}, bf16[128,768]{1,0:T(8,128)(2,1)}, u32[]{:S(2)}, u32[]{:S(2)}) collective-permute-start(bf16[128,768]{1,0:T(8,128)(2,1)} %collective-permute-done.28), channel_id=1, source_target_pairs={{0,15},{1,0},{2,1},{3,2},{4,3},{5,4},{6,5},{7,6},{8,7},{9,8},{10,9... | collective-permute-start | bytes 589832 | tf_op jit(solution)/shard_map/ppermute | solution.py:22
  159.7 36.0 %collective-permute-start.22 = (bf16[128,768]{1,0:T(8,128)(2,1)}, bf16[128,768]{1,0:T(8,128)(2,1)}, u32[]{:S(2)}, u32[]{:S(2)}) collective-permute-start(bf16[128,768]{1,0:T(8,128)(2,1)} %collective-permute-done.21), channel_id=1, source_target_pairs={{0,1},{1,2},{2,3},{3,4},{4,5},{5,6},{6,7},{7,8},{8,9},{9,10},{10,1... | collective-permute-start | bytes 589832 | tf_op jit(solution)/shard_map/ppermute | solution.py:20
  188.5 48.1 %all-to-all-start.2 = ((bf16[16,768,128]{1,2,0:T(8,128)(2,1)}), bf16[16,768,128]{1,2,0:T(8,128)(2,1)}, u32[]{:S(2)}, u32[]{:S(2)}) async-start(bf16[16,768,128]{1,2,0:T(8,128)(2,1)} %convert_element_type.124), calls=%async_computation.2 | async-start | bytes 6291456 | tf_op jit(solution)/shard_map/all_to_all | solution.py:127
  263.9 20.3 %all-to-all-start.3 = ((bf16[16,256,128]{1,2,0:T(8,128)(2,1)}), bf16[16,256,128]{1,2,0:T(8,128)(2,1)}, u32[]{:S(2)}, u32[]{:S(2)}) async-start(bf16[16,256,128]{1,2,0:T(8,128)(2,1)} %bitcast.171), calls=%async_computation.3 | async-start | bytes 2097152 | tf_op jit(solution)/shard_map/all_to_all | solution.py:109
  271.3 78.3 %all-reduce.8.cloned.1.call-start = ((), (), s32[]{:S(2)}) async-start(), calls=%async_computation.12 | async-start | bytes 1048576 | tf_op jit(solution)/shard_map/psum | solution.py:47
  287.1 87.8 %all-gather.6.cloned.1.call-start = ((), (), s32[]{:S(2)}) async-start(), calls=%async_computation.11 | async-start | bytes 1179648 | tf_op jit(solution)/shard_map/all_gather | solution.py:43
  352.2 22.0 %all-to-all-start.4 = ((bf16[16,256,128]{1,2,0:T(8,128)(2,1)}), bf16[16,256,128]{1,2,0:T(8,128)(2,1)S(1)}, u32[]{:S(2)}, u32[]{:S(2)}) async-start(bf16[16,256,128]{1,2,0:T(8,128)(2,1)} %bitcast.170), calls=%async_computation.4 | async-start | bytes 2097152 | tf_op jit(solution)/shard_map/all_to_all | solution.py:127
  395.7 20.1 %all-to-all-start.5 = ((bf16[16,256,128]{1,2,0:T(8,128)(2,1)}), bf16[16,256,128]{1,2,0:T(8,128)(2,1)}, u32[]{:S(2)}, u32[]{:S(2)}) async-start(bf16[16,256,128]{1,2,0:T(8,128)(2,1)} %bitcast.42), calls=%async_computation.5 | async-start | bytes 2097152 | tf_op jit(solution)/shard_map/all_to_all | solution.py:109
  400.2 77.5 %all-reduce.10.cloned.1.call-start = ((), (), s32[]{:S(2)}) async-start(), calls=%async_computation.14 | async-start | bytes 1048576 | tf_op jit(solution)/shard_map/psum | solution.py:47
  418.7 71.6 %collective-permute-start.45 = (bf16[128,1024]{1,0:T(8,128)(2,1)S(1)}, bf16[128,1024]{1,0:T(8,128)(2,1)S(1)}, u32[]{:S(2)}, u32[]{:S(2)}) collective-permute-start(bf16[128,1024]{1,0:T(8,128)(2,1)S(1)} %copy-done.23), channel_id=1, source_target_pairs={{0,1},{1,2},{2,3},{3,4},{4,5},{5,6},{6,7},{7,8},{8,9},{9,10},{10,1... | collective-permute-start | bytes 786440 | tf_op jit(solution)/shard_map/ppermute | solution.py:20
  483.4 137.7 %all-to-all-start.6 = ((bf16[16,1024,128]{1,2,0:T(8,128)(2,1)}), bf16[16,1024,128]{1,2,0:T(8,128)(2,1)}, u32[]{:S(2)}, u32[]{:S(2)}) async-start(bf16[16,1024,128]{1,2,0:T(8,128)(2,1)} %bitcast.164), calls=%async_computation.6 | async-start | bytes 8388608 | tf_op jit(solution)/shard_map/all_to_all | solution.py:127
  490.3 140.2 %all-gather.8.cloned.1.call-start = ((), (), s32[]{:S(2)}) async-start(), calls=%async_computation.13 | async-start | bytes 1179648 | tf_op jit(solution)/shard_map/all_gather | solution.py:43
  490.3 55.6 %collective-permute-start.46 = (bf16[128,1024]{1,0:T(8,128)(2,1)S(1)}, bf16[128,1024]{1,0:T(8,128)(2,1)S(1)}, u32[]{:S(2)}, u32[]{:S(2)}) collective-permute-start(bf16[128,1024]{1,0:T(8,128)(2,1)S(1)} %collective-permute-done.45), channel_id=1, source_target_pairs={{0,1},{1,2},{2,3},{3,4},{4,5},{5,6},{6,7},{7,8},{8,9},{9,10},{10,1... | collective-permute-start | bytes 786440 | tf_op jit(solution)/shard_map/ppermute | solution.py:20
  492.3 53.6 %collective-permute-start.53 = (bf16[128,1024]{1,0:T(8,128)(2,1)S(1)}, bf16[128,1024]{1,0:T(8,128)(2,1)S(1)}, u32[]{:S(2)}, u32[]{:S(2)}) collective-permute-start(bf16[128,1024]{1,0:T(8,128)(2,1)S(1)} %copy-done.23), channel_id=1, source_target_pairs={{0,15},{1,0},{2,1},{3,2},{4,3},{5,4},{6,5},{7,6},{8,7},{9,8},{10,9... | collective-permute-start | bytes 786440 | tf_op jit(solution)/shard_map/ppermute | solution.py:22
  599.9 20.6 %collective-permute-start.59 = (bf16[128,1024]{1,0:T(8,128)(2,1)S(1)}, bf16[128,1024]{1,0:T(8,128)(2,1)S(1)}, u32[]{:S(2)}, u32[]{:S(2)}) collective-permute-start(bf16[128,1024]{1,0:T(8,128)(2,1)S(1)} %collective-permute-done.58), channel_id=1, source_target_pairs={{0,15},{1,0},{2,1},{3,2},{4,3},{5,4},{6,5},{7,6},{8,7},{9,8},{10,9... | collective-permute-start | bytes 786440 | tf_op jit(solution)/shard_map/ppermute | solution.py:22
  641.4 147.3 %all-to-all-start.7 = ((bf16[16,1024,128]{1,2,0:T(8,128)(2,1)}), bf16[16,1024,128]{1,2,0:T(8,128)(2,1)}, u32[]{:S(2)}, u32[]{:S(2)}) async-start(bf16[16,1024,128]{1,2,0:T(8,128)(2,1)} %bitcast.165), calls=%async_computation.7 | async-start | bytes 8388608 | tf_op jit(solution)/shard_map/all_to_all | solution.py:109
  648.4 203.3 %all-reduce.12.cloned.1.call-start = ((), (), s32[]{:S(2)}) async-start(), calls=%async_computation.15 | async-start | bytes 1048576 | tf_op jit(solution)/shard_map/psum | solution.py:47
  648.4 59.2 %collective-permute-start.30 = (bf16[128,1024]{1,0:T(8,128)(2,1)S(1)}, bf16[128,1024]{1,0:T(8,128)(2,1)S(1)}, u32[]{:S(2)}, u32[]{:S(2)}) collective-permute-start(bf16[128,1024]{1,0:T(8,128)(2,1)S(1)} %copy-done.24), channel_id=1, source_target_pairs={{0,1},{1,2},{2,3},{3,4},{4,5},{5,6},{6,7},{7,8},{8,9},{9,10},{10,1... | collective-permute-start | bytes 786440 | tf_op jit(solution)/shard_map/ppermute | solution.py:20
  771.8 94.1 %collective-permute-start.44 = (bf16[128,1024]{1,0:T(8,128)(2,1)}, bf16[128,1024]{1,0:T(8,128)(2,1)}, u32[]{:S(2)}, u32[]{:S(2)}) collective-permute-start(bf16[128,1024]{1,0:T(8,128)(2,1)} %collective-permute-done.43), channel_id=1, source_target_pairs={{0,15},{1,0},{2,1},{3,2},{4,3},{5,4},{6,5},{7,6},{8,7},{9,8},{10,9... | collective-permute-start | bytes 786440 | tf_op jit(solution)/shard_map/ppermute | solution.py:22
  854.2 22.1 %all-to-all-start.8 = ((bf16[16,256,128]{1,2,0:T(8,128)(2,1)}), bf16[16,256,128]{1,2,0:T(8,128)(2,1)}, u32[]{:S(2)}, u32[]{:S(2)}) async-start(bf16[16,256,128]{1,2,0:T(8,128)(2,1)} %bitcast.60), calls=%async_computation.8 | async-start | bytes 2097152 | tf_op jit(solution)/shard_map/all_to_all | solution.py:127
  861.1 80.4 %all-reduce.14.cloned.1.call-start = ((), (), s32[]{:S(2)}) async-start(), calls=%async_computation.16 | async-start | bytes 2097152 | tf_op jit(solution)/shard_map/psum | solution.py:47
  (102 other events, 2447.2 us)
Sparse Core Ops, SparseCore 0:
  52.4 64.0 all-reduce.5
  118.3 22.4 all-gather.3
  287.2 62.3 all-reduce.7
  351.2 22.4 all-gather.5
  418.8 58.8 all-reduce.9
  611.9 18.5 all-gather.7
  794.4 57.2 all-reduce.11
  879.7 61.7 all-reduce.13
